TPU v7x, 32 devices: a whole 2x2x4 slice. The times are simulated.
32 devices in a mesh: groups: 2 (over x), row: 8 (over z, y), col: 2 (over core).
Axes of the slice: x: 2, y: 2, z: 4, core: 2. Of those that a mesh axis runs over, the one named last changes fastest.
Arguments:
- pair_repr: bfloat16 [64, 32, 128], P(('groups', 'row'), 'col'), parts along dimension 0, may hold values from -6 to 6
- in_gain: float32 [128], replicated, may hold values from 0.5 to 1.5
- in_bias: float32 [128], replicated, may hold values from -0.5 to 0.5
- left_gate_w: bfloat16 [128, 128], replicated, may hold values from -0.5 to 0.5
- left_w: bfloat16 [128, 128], replicated, may hold values from -0.5 to 0.5
- right_gate_w: bfloat16 [128, 128], replicated, may hold values from -0.5 to 0.5
- right_w: bfloat16 [128, 128], replicated, may hold values from -0.5 to 0.5
- out_gate_w: bfloat16 [128, 128], replicated, may hold values from -0.5 to 0.5
- mid_gain: float32 [128], replicated, may hold values from 0.5 to 1.5
- mid_bias: float32 [128], replicated, may hold values from -0.5 to 0.5
- out_w: bfloat16 [128, 128], replicated, may hold values from -0.5 to 0.5
Outputs:
- update: bfloat16 [64, 32, 128], P(('groups', 'row'), 'col'), parts along dimension 0
There are 2 independent parts, one for each index of `groups`. A program takes and returns all parts, laid end to end along the dimension named above; an argument that names none is the same for every part. Nothing has to cross between parts.
All inputs are finite; a program needn't handle non-finite values.
Results may differ from a plain program's by a relative error of at most 0.015.
Values may be sent and summed in bfloat16 or wider, within the bound.
A program may use at most 64 MiB of HBM per device.

v0:
```python
import jax
import jax.numpy as jnp
from jax import lax
from jax.sharding import PartitionSpec as P


def layer_norm(values, norm_gain, norm_bias):
    average = jnp.mean(values, axis=-1, keepdims=True)
    centred = values - average
    variance = jnp.mean(centred * centred, axis=-1, keepdims=True)
    return centred / jnp.sqrt(variance + 1e-05) * norm_gain + norm_bias


def on_device(
    pair_repr,
    in_gain,
    in_bias,
    left_gate_w,
    left_w,
    right_gate_w,
    right_w,
    out_gate_w,
    mid_gain,
    mid_bias,
    out_w,
):
    row_count, col_count, channels = pair_repr.shape
    hidden = left_w.shape[1]
    normed = layer_norm(pair_repr.astype(jnp.float32), in_gain, in_bias).astype(jnp.bfloat16)
    flattened = normed.reshape(row_count * col_count, channels)
    left_side = (
        (
            jax.nn.sigmoid(jnp.dot(flattened, left_gate_w, preferred_element_type=jnp.float32))
            * jnp.dot(flattened, left_w, preferred_element_type=jnp.float32)
        )
        .astype(jnp.bfloat16)
        .reshape(row_count, col_count, hidden)
    )
    right_side = (
        (
            jax.nn.sigmoid(jnp.dot(flattened, right_gate_w, preferred_element_type=jnp.float32))
            * jnp.dot(flattened, right_w, preferred_element_type=jnp.float32)
        )
        .astype(jnp.bfloat16)
        .reshape(row_count, col_count, hidden)
    )
    gating = jax.nn.sigmoid(jnp.dot(flattened, out_gate_w, preferred_element_type=jnp.float32))
    left_full = lax.all_gather(left_side, "col", axis=1, tiled=True)
    right_all = lax.all_gather(right_side, "row", axis=0, tiled=True)
    right_mine = lax.all_to_all(right_all, "col", split_axis=0, concat_axis=1, tiled=True)
    triangle = jnp.einsum("ikh,jkh->ijh", left_full, right_mine, preferred_element_type=jnp.float32)
    middle = (
        layer_norm(triangle, mid_gain, mid_bias)
        .astype(jnp.bfloat16)
        .reshape(row_count * col_count, hidden)
    )
    result = gating * jnp.dot(middle, out_w, preferred_element_type=jnp.float32)
    return result.astype(jnp.bfloat16).reshape(row_count, col_count, channels)


def solution(mesh):
    in_specs = (P(("groups", "row"), "col", None), P(), P(), P(), P(), P(), P(), P(), P(), P(), P())
    out_specs = P(("groups", "row"), "col", None)
    return jax.shard_map(
        on_device, mesh=mesh, in_specs=in_specs, out_specs=out_specs, check_vma=False
    )
```

profile of v0, /device:TPU:0, one launch (start us, length us, event | category | flops | bytes accessed | tf_op | source)
XLA Modules:
  0.0 45.9 jit_solution(8318891046903231604)
XLA Ops:
  0.0 0.0 copy-start
  0.0 0.0 copy-start.1
  0.0 0.9 %convert_reduce_fusion = f32[4,16]{1,0:T(4,128)S(1)} fusion(bf16[4,16,128]{2,1,0:T(8,128)(2,1)} %param.11), kind=kLoop, calls=%fused_computation.19 | loop fusion | flops 16320 | bytes 16640 | tf_op jit(solution)/shard_map/reduce_sum | solution.py:8
  0.9 0.0 copy-done.1
  0.9 0.2 fusion.14
  1.0 0.0 copy-start.5
  1.1 0.0 copy-start.6
  1.1 0.6 %copy-done.5 = f32[128]{0:T(128)S(1)} copy-done((f32[128]{0:T(128)S(1)}, f32[128]{0:T(128)}, u32[]{:S(2)}) %copy-start.5) | copy-done | bytes 536
  1.7 0.0 copy-done.6
  1.7 0.1 fusion.17
  1.8 0.0 copy-done
  1.8 0.0 copy-start.2
  1.8 0.1 fusion.5
  2.0 0.6 %copy-done.2 = bf16[128,128]{1,0:T(8,128)(2,1)S(1)} copy-done((bf16[128,128]{1,0:T(8,128)(2,1)S(1)}, bf16[128,128]{1,0:T(8,128)(2,1)}, u32[]{:S(2)}) %copy-start.2) | copy-done | bytes 32792
  2.6 0.1 fusion.9
  2.7 32.3 %all_gather.6 = bf16[32,16,128]{2,1,0:T(8,128)(2,1)S(1)} all-gather(bf16[4,16,128]{2,1,0:T(8,128)(2,1)S(1)} %bitcast.37), channel_id=1, replica_groups=mesh['groups'=2,'row'=8,'col'=2] {'row'}, dimensions={0}, use_global_device_ids=true | all-gather | bytes 147456 | tf_op jit(solution)/shard_map/all_gather | solution.py:49
  35.0 3.8 %all_to_all.18 = bf16[32,16,128]{2,1,0:T(8,128)(2,1)S(1)} all-to-all(bf16[32,16,128]{2,1,0:T(8,128)(2,1)S(1)} %all_gather.6), channel_id=1, replica_groups=mesh['groups'=2,'row'=8,'col'=2] {'col'}, dimensions={0} | all-to-all | bytes 262144 | tf_op jit(solution)/shard_map/all_to_all | solution.py:50
  38.9 0.0 copy-start.9
  38.9 0.4 copy.28
  39.3 0.3 copy-done.9
  39.6 0.0 copy-start.3
  39.6 0.1 fusion.2
  39.8 0.6 %copy-done.3 = bf16[128,128]{1,0:T(8,128)(2,1)S(1)} copy-done((bf16[128,128]{1,0:T(8,128)(2,1)S(1)}, bf16[128,128]{1,0:T(8,128)(2,1)}, u32[]{:S(2)}) %copy-start.3) | copy-done | bytes 32792
  40.4 0.1 fusion.10
  40.5 1.8 %all_gather.7 = bf16[4,32,128]{2,0,1:T(4,128)(2,1)S(1)} all-gather(bf16[4,16,128]{2,0,1:T(4,128)(2,1)S(1)} %copy.27), channel_id=1, replica_groups=mesh['groups'=2,'row'=8,'col'=2] {'col'}, dimensions={1}, use_global_device_ids=true | all-gather | bytes 49152 | tf_op jit(solution)/shard_map/all_gather | solution.py:48
  42.4 0.1 copy.29
  42.5 0.4 fusion.18
  42.9 0.1 copy.30
  43.0 0.0 copy-start.10
  43.0 0.1 bitcast_reduce_fusion
  43.1 0.2 multiply_reduce_fusion
  43.3 0.5 %copy-done.10 = bf16[128,128]{1,0:T(8,128)(2,1)S(1)} copy-done((bf16[128,128]{1,0:T(8,128)(2,1)S(1)}, bf16[128,128]{1,0:T(8,128)(2,1)}, u32[]{:S(2)}) %copy-start.10) | copy-done | bytes 32792
  43.8 0.0 copy-start.7
  43.8 0.0 copy-start.8
  43.8 0.1 fusion.8
  43.9 0.5 %copy-done.7 = f32[128]{0:T(128)S(1)} copy-done((f32[128]{0:T(128)S(1)}, f32[128]{0:T(128)}, u32[]{:S(2)}) %copy-start.7) | copy-done | bytes 536
  44.4 0.0 copy-done.8
  44.4 0.0 copy-start.4
  44.4 0.1 add_convert_fusion
  44.5 0.7 %copy-done.4 = bf16[128,128]{1,0:T(8,128)(2,1)S(1)} copy-done((bf16[128,128]{1,0:T(8,128)(2,1)S(1)}, bf16[128,128]{1,0:T(8,128)(2,1)}, u32[]{:S(2)}) %copy-start.4) | copy-done | bytes 32792
  45.2 0.7 %fusion.11 = bf16[64,128]{1,0:T(8,128)(2,1)} fusion(f32[64,128]{1,0:T(8,128)S(1)} %fusion.8, bf16[64,128]{1,0:T(8,128)(2,1)S(1)} %bitcast.38, bf16[128,128]{1,0:T(8,128)(2,1)S(1)} %copy-done.4), kind=kOutput, calls=%fused_computation.17 | convolution fusion | flops 2113536 | bytes 98304 | tf_op jit(solution)/shard_map/dot_general | solution.py:57
  (6 shorter events, 0.1 us)
Async XLA Ops:
  0.0 1.8 %copy-start = (bf16[128,128]{1,0:T(8,128)(2,1)S(1)}, bf16[128,128]{1,0:T(8,128)(2,1)}, u32[]{:S(2)}) copy-start(bf16[128,128]{1,0:T(8,128)(2,1)} %param.16) | copy-start | bytes 98308
  0.0 0.9 %copy-start.1 = (bf16[4,16,128]{2,1,0:T(8,128)(2,1)S(1)}, bf16[4,16,128]{2,1,0:T(8,128)(2,1)}, u32[]{:S(2)}) copy-start(bf16[4,16,128]{2,1,0:T(8,128)(2,1)} %param.11) | copy-start | bytes 49156
  1.0 0.7 %copy-start.5 = (f32[128]{0:T(128)S(1)}, f32[128]{0:T(128)}, u32[]{:S(2)}) copy-start(f32[128]{0:T(128)} %param.13) | copy-start | bytes 1540
  1.1 0.7 %copy-start.6 = (f32[128]{0:T(128)S(1)}, f32[128]{0:T(128)}, u32[]{:S(2)}) copy-start(f32[128]{0:T(128)} %param.12) | copy-start | bytes 1540
  1.8 0.8 %copy-start.2 = (bf16[128,128]{1,0:T(8,128)(2,1)S(1)}, bf16[128,128]{1,0:T(8,128)(2,1)}, u32[]{:S(2)}) copy-start(bf16[128,128]{1,0:T(8,128)(2,1)} %param.17) | copy-start | bytes 98308
  38.9 0.8 %copy-start.9 = (bf16[128,128]{1,0:T(8,128)(2,1)S(1)}, bf16[128,128]{1,0:T(8,128)(2,1)}, u32[]{:S(2)}) copy-start(bf16[128,128]{1,0:T(8,128)(2,1)} %param.14) | copy-start | bytes 98308
  39.6 0.8 %copy-start.3 = (bf16[128,128]{1,0:T(8,128)(2,1)S(1)}, bf16[128,128]{1,0:T(8,128)(2,1)}, u32[]{:S(2)}) copy-start(bf16[128,128]{1,0:T(8,128)(2,1)} %param.15) | copy-start | bytes 98308
  43.0 0.8 %copy-start.10 = (bf16[128,128]{1,0:T(8,128)(2,1)S(1)}, bf16[128,128]{1,0:T(8,128)(2,1)}, u32[]{:S(2)}) copy-start(bf16[128,128]{1,0:T(8,128)(2,1)} %param.18) | copy-start | bytes 98308
  43.8 0.7 %copy-start.7 = (f32[128]{0:T(128)S(1)}, f32[128]{0:T(128)}, u32[]{:S(2)}) copy-start(f32[128]{0:T(128)} %param.20) | copy-start | bytes 1540
  43.8 0.7 %copy-start.8 = (f32[128]{0:T(128)S(1)}, f32[128]{0:T(128)}, u32[]{:S(2)}) copy-start(f32[128]{0:T(128)} %param.19) | copy-start | bytes 1540
  44.4 0.8 %copy-start.4 = (bf16[128,128]{1,0:T(8,128)(2,1)S(1)}, bf16[128,128]{1,0:T(8,128)(2,1)}, u32[]{:S(2)}) copy-start(bf16[128,128]{1,0:T(8,128)(2,1)} %param.21) | copy-start | bytes 98308
where the time goes:
time: 46.5 us; the launch traced here: 45.9 us
  blocking collectives  38 us (82%)
  local copies, waits for them, and re-layouts  4.56 us (10%)
  matrix products  1.79 us (4%)
  other arithmetic  1.48 us (3%)
    all_gather x1, blocking collectives, on_device(): right_all = lax.all_gather(right_side, 'row', axis=0, tiled=True)  32.3 us
    unnamed x22, local copies, waits for them, and re-layouts  3.86 us
    all_to_all x1, blocking collectives, on_device(): lax.all_to_all(right_all, 'col', split_axis=0, concat_axis=1, tiled=True)  3.83 us
    all_gather x1, blocking collectives, on_device(): left_full = lax.all_gather(left_side, 'col', axis=1, tiled=True)  1.83 us
    reduce_sum x2, other arithmetic, layer_norm(): average = jnp.mean(values, axis=-1, keepdims=True)  0.96 us

commit v1 on v0

--- a/solution.py
+++ b/solution.py
@@ -46,7 +46,16 @@
     )
     gating = jax.nn.sigmoid(jnp.dot(flattened, out_gate_w, preferred_element_type=jnp.float32))
     left_full = lax.all_gather(left_side, "col", axis=1, tiled=True)
-    right_all = lax.all_gather(right_side, "row", axis=0, tiled=True)
+    ways = lax.axis_size("row")
+    up = [(d, (d + 1) % ways) for d in range(ways)]
+    down = [(d, (d - 1) % ways) for d in range(ways)]
+    earlier, later = ([right_side], [right_side])
+    for _ in range(ways // 2):
+        earlier.append(lax.ppermute(earlier[-1], "row", up))
+    for _ in range((ways - 1) // 2):
+        later.append(lax.ppermute(later[-1], "row", down))
+    line = jnp.concatenate([*earlier[::-1], *later[1:]], axis=0)
+    right_all = jnp.roll(line, (lax.axis_index("row") - ways // 2) * right_side.shape[0], axis=0)
     right_mine = lax.all_to_all(right_all, "col", split_axis=0, concat_axis=1, tiled=True)
     triangle = jnp.einsum("ikh,jkh->ijh", left_full, right_mine, preferred_element_type=jnp.float32)
     middle = (

time: 46.5 us -> 38.8 us (0.83)
  blocking collectives: 38 us -> 5.67 us
  starting transfers between devices: 0 us -> 15.6 us
  waiting for transfers between devices: 0 us -> 10.9 us
  local copies, waits for them, and re-layouts: 4.56 us -> 2.8 us
    all_gather x1 -> x0, blocking collectives: 32.3 us -> none  [on_device(): right_all = lax.all_gather(right_side, 'row', axis=0, tiled=True)]
    ppermute x0 -> x7, starting transfers between devices: none -> 15.6 us  [the longest x3 12.6 us: on_device(): later.append(lax.ppermute(later[-1], 'row', down))]
    ppermute x0 -> x7, waiting for transfers between devices: none -> 10.9 us  [the longest x4 9.49 us: on_device(): earlier.append(lax.ppermute(earlier[-1], 'row', up))]
    unnamed x22 -> x37, local copies, waits for them, and re-layouts: 3.86 us -> 2.07 us
  transfers between devices with their start and end apart: 0 -> 7, of which waited for: 0 -> 4; matrix products, arithmetic and copies ran while one was open for 0% -> 2% of each run, Pallas kernels for 0% -> 0%
where the time goes in v1:
time: 38.8 us; the launch traced here: 38.4 us
  starting transfers between devices  15.6 us (40%)
  waiting for transfers between devices  10.9 us (28%)
  blocking collectives  5.67 us (15%)
  local copies, waits for them, and re-layouts  2.8 us (7%)
  matrix products  1.8 us (5%)
  other arithmetic  1.49 us (4%)
    ppermute x3, starting transfers between devices, on_device(): later.append(lax.ppermute(later[-1], 'row', down))  12.6 us
    ppermute x4, waiting for transfers between devices, on_device(): earlier.append(lax.ppermute(earlier[-1], 'row', up))  9.49 us
    all_to_all x1, blocking collectives, on_device(): lax.all_to_all(right_all, 'col', split_axis=0, concat_axis=1, tiled=True)  3.84 us
    ppermute x4, starting transfers between devices, on_device(): earlier.append(lax.ppermute(earlier[-1], 'row', up))  2.98 us
    unnamed x37, local copies, waits for them, and re-layouts  2.07 us
    all_gather x1, blocking collectives, on_device(): left_full = lax.all_gather(left_side, 'col', axis=1, tiled=True)  1.83 us
    ppermute x3, waiting for transfers between devices, on_device(): later.append(lax.ppermute(later[-1], 'row', down))  1.37 us
    reduce_sum x2, other arithmetic, layer_norm(): average = jnp.mean(values, axis=-1, keepdims=True)  0.98 us
  transfers between devices with their start and end apart: 7, of which 4 were waited for; matrix products, arithmetic and copies ran while one was open for 2% of the time, Pallas kernels for 0%

profile of v1, /device:TPU:0, one launch (start us, length us, event | category | flops | bytes accessed | tf_op | source)
XLA Modules:
  0.0 38.4 jit_solution(7618780797933543358)
XLA Ops:
  0.0 0.0 copy-start
  0.0 0.0 copy-start.1
  0.0 0.9 %convert_reduce_fusion = f32[4,16]{1,0:T(4,128)S(1)} fusion(bf16[4,16,128]{2,1,0:T(8,128)(2,1)} %param.11), kind=kLoop, calls=%fused_computation.19 | loop fusion | flops 16320 | bytes 16640 | tf_op jit(solution)/shard_map/reduce_sum | solution.py:8
  0.9 0.0 copy-done.1
  0.9 0.2 fusion.14
  1.0 0.0 copy-start.5
  1.1 0.0 copy-start.6
  1.1 0.6 %copy-done.5 = f32[128]{0:T(128)S(1)} copy-done((f32[128]{0:T(128)S(1)}, f32[128]{0:T(128)}, u32[]{:S(2)}) %copy-start.5) | copy-done | bytes 536
  1.7 0.0 copy-done.6
  1.7 0.1 fusion.17
  1.8 0.0 copy-done
  1.8 0.0 copy-start.2
  1.8 0.1 fusion.5
  2.0 0.6 %copy-done.2 = bf16[128,128]{1,0:T(8,128)(2,1)S(1)} copy-done((bf16[128,128]{1,0:T(8,128)(2,1)S(1)}, bf16[128,128]{1,0:T(8,128)(2,1)}, u32[]{:S(2)}) %copy-start.2) | copy-done | bytes 32792
  2.6 0.0 copy-start.9
  2.6 0.1 fusion.9
  2.7 0.0 copy-start.3
  2.7 3.0 %collective-permute-start = (bf16[4,16,128]{2,1,0:T(8,128)(2,1)S(1)}, bf16[4,16,128]{2,1,0:T(8,128)(2,1)S(1)}, u32[]{:S(2)}, u32[]{:S(2)}) collective-permute-start(bf16[4,16,128]{2,1,0:T(8,128)(2,1)S(1)} %bitcast.32), channel_id=1, source_target_pairs={{0,2},{2,4},{4,6},{6,8},{8,10},{10,12},{12,14},{14,0},{1,3},{3,5},... | collective-permute-start | bytes 49160 | tf_op jit(solution)/shard_map/ppermute | solution.py:54
  5.7 3.1 %collective-permute-start.4 = (bf16[4,16,128]{2,1,0:T(8,128)(2,1)S(1)}, bf16[4,16,128]{2,1,0:T(8,128)(2,1)S(1)}, u32[]{:S(2)}, u32[]{:S(2)}) collective-permute-start(bf16[4,16,128]{2,1,0:T(8,128)(2,1)S(1)} %bitcast.33), channel_id=1, source_target_pairs={{0,14},{2,0},{4,2},{6,4},{8,6},{10,8},{12,10},{14,12},{1,15},{3,1}... | collective-permute-start | bytes 49160 | tf_op jit(solution)/shard_map/ppermute | solution.py:56
  8.8 1.7 %collective-permute-done = bf16[4,16,128]{2,1,0:T(8,128)(2,1)S(1)} collective-permute-done((bf16[4,16,128]{2,1,0:T(8,128)(2,1)S(1)}, bf16[4,16,128]{2,1,0:T(8,128)(2,1)S(1)}, u32[]{:S(2)}, u32[]{:S(2)}) %collective-permute-start) | collective-permute-done | bytes 16416 | tf_op jit(solution)/shard_map/ppermute | solution.py:54
  10.5 0.0 collective-permute-start.1
  10.5 0.0 copy-done.9
  10.5 0.1 fusion.2
  10.6 0.0 copy-start.10
  10.6 6.3 %collective-permute-done.1 = bf16[4,16,128]{2,1,0:T(8,128)(2,1)S(1)} collective-permute-done((bf16[4,16,128]{2,1,0:T(8,128)(2,1)S(1)}, bf16[4,16,128]{2,1,0:T(8,128)(2,1)S(1)}, u32[]{:S(2)}, u32[]{:S(2)}) %collective-permute-start.1) | collective-permute-done | bytes 16416 | tf_op jit(solution)/shard_map/ppermute | solution.py:54
  16.9 0.0 collective-permute-start.2
  16.9 0.0 copy-done.3
  16.9 0.1 fusion.10
  17.0 0.0 collective-permute-done.4
  17.0 4.7 %collective-permute-start.5 = (bf16[4,16,128]{2,1,0:T(8,128)(2,1)S(1)}, bf16[4,16,128]{2,1,0:T(8,128)(2,1)S(1)}, u32[]{:S(2)}, u32[]{:S(2)}) collective-permute-start(bf16[4,16,128]{2,1,0:T(8,128)(2,1)S(1)} %collective-permute-done.4), channel_id=1, source_target_pairs={{0,14},{2,0},{4,2},{6,4},{8,6},{10,8},{12,10},{14,12},{1,15},{3,1}... | collective-permute-start | bytes 49160 | tf_op jit(solution)/shard_map/ppermute | solution.py:56
  21.8 1.6 %collective-permute-done.2 = bf16[4,16,128]{2,1,0:T(8,128)(2,1)S(1)} collective-permute-done((bf16[4,16,128]{2,1,0:T(8,128)(2,1)S(1)}, bf16[4,16,128]{2,1,0:T(8,128)(2,1)S(1)}, u32[]{:S(2)}, u32[]{:S(2)}) %collective-permute-start.2) | collective-permute-done | bytes 16416 | tf_op jit(solution)/shard_map/ppermute | solution.py:54
  23.3 0.0 collective-permute-start.3
  23.3 0.0 copy-done.10
  23.3 0.1 fusion.8
  23.5 1.8 %all_gather.3 = bf16[4,32,128]{2,0,1:T(4,128)(2,1)S(1)} all-gather(bf16[4,16,128]{2,0,1:T(4,128)(2,1)S(1)} %copy.27), channel_id=1, replica_groups=mesh['groups'=2,'row'=8,'col'=2] {'col'}, dimensions={1}, use_global_device_ids=true | all-gather | bytes 49152 | tf_op jit(solution)/shard_map/all_gather | solution.py:48
  25.4 0.1 copy.29
  25.5 0.0 collective-permute-done.5
  25.5 4.8 %collective-permute-start.6 = (bf16[4,16,128]{2,1,0:T(8,128)(2,1)S(1)}, bf16[4,16,128]{2,1,0:T(8,128)(2,1)S(1)}, u32[]{:S(2)}, u32[]{:S(2)}) collective-permute-start(bf16[4,16,128]{2,1,0:T(8,128)(2,1)S(1)} %collective-permute-done.5), channel_id=1, source_target_pairs={{0,14},{2,0},{4,2},{6,4},{8,6},{10,8},{12,10},{14,12},{1,15},{3,1}... | collective-permute-start | bytes 49160 | tf_op jit(solution)/shard_map/ppermute | solution.py:56
  30.3 0.0 collective-permute-done.3
  30.4 1.4 %collective-permute-done.6 = bf16[4,16,128]{2,1,0:T(8,128)(2,1)S(1)} collective-permute-done((bf16[4,16,128]{2,1,0:T(8,128)(2,1)S(1)}, bf16[4,16,128]{2,1,0:T(8,128)(2,1)S(1)}, u32[]{:S(2)}, u32[]{:S(2)}) %collective-permute-start.6) | collective-permute-done | bytes 16416 | tf_op jit(solution)/shard_map/ppermute | solution.py:56
  31.9 3.8 %all_to_all.18 = bf16[32,16,128]{2,1,0:T(8,128)(2,1)S(1)} all-to-all(bf16[32,16,128]{2,1,0:T(8,128)(2,1)S(1)} %constant_dynamic-slice_fusion), channel_id=1, replica_groups=mesh['groups'=2,'row'=8,'col'=2] {'col'}, dimensions={0} | all-to-all | bytes 262144 | tf_op jit(solution)/shard_map/all_to_all | solution.py:59
  35.7 0.4 %copy.28 = bf16[16,32,128]{1,0,2:T(8,128)(2,1)S(1)} copy(bf16[16,32,128]{2,1,0:T(8,128)(2,1)S(1)} %bitcast.30) | data formatting | bytes 262144 | tf_op jit(solution)/shard_map/all_to_all | solution.py:59
  36.2 0.4 fusion.18
  36.5 0.1 copy.30
  36.6 0.0 copy-start.7
  36.6 0.0 copy-start.8
  36.6 0.1 bitcast_reduce_fusion
  36.7 0.2 multiply_reduce_fusion
  36.9 0.0 copy-start.4
  36.9 0.4 copy-done.7
  37.3 0.0 copy-done.8
  37.3 0.1 add_convert_fusion
  37.4 0.3 copy-done.4
  37.7 0.7 %fusion.11 = bf16[64,128]{1,0:T(8,128)(2,1)} fusion(f32[64,128]{1,0:T(8,128)S(1)} %fusion.8, bf16[64,128]{1,0:T(8,128)(2,1)S(1)} %bitcast.42, bf16[128,128]{1,0:T(8,128)(2,1)S(1)} %copy-done.4), kind=kOutput, calls=%fused_computation.17 | convolution fusion | flops 2113536 | bytes 98304 | tf_op jit(solution)/shard_map/dot_general | solution.py:66
  (23 shorter events, 0.2 us)
Async XLA Ops:
  0.0 1.8 %copy-start = (bf16[128,128]{1,0:T(8,128)(2,1)S(1)}, bf16[128,128]{1,0:T(8,128)(2,1)}, u32[]{:S(2)}) copy-start(bf16[128,128]{1,0:T(8,128)(2,1)} %param.16) | copy-start | bytes 98308
  0.0 0.9 %copy-start.1 = (bf16[4,16,128]{2,1,0:T(8,128)(2,1)S(1)}, bf16[4,16,128]{2,1,0:T(8,128)(2,1)}, u32[]{:S(2)}) copy-start(bf16[4,16,128]{2,1,0:T(8,128)(2,1)} %param.11) | copy-start | bytes 49156
  1.0 0.7 %copy-start.5 = (f32[128]{0:T(128)S(1)}, f32[128]{0:T(128)}, u32[]{:S(2)}) copy-start(f32[128]{0:T(128)} %param.13) | copy-start | bytes 1540
  1.1 0.7 %copy-start.6 = (f32[128]{0:T(128)S(1)}, f32[128]{0:T(128)}, u32[]{:S(2)}) copy-start(f32[128]{0:T(128)} %param.12) | copy-start | bytes 1540
  1.8 0.8 %copy-start.2 = (bf16[128,128]{1,0:T(8,128)(2,1)S(1)}, bf16[128,128]{1,0:T(8,128)(2,1)}, u32[]{:S(2)}) copy-start(bf16[128,128]{1,0:T(8,128)(2,1)} %param.17) | copy-start | bytes 98308
  2.6 7.9 %copy-start.9 = (bf16[128,128]{1,0:T(8,128)(2,1)S(1)}, bf16[128,128]{1,0:T(8,128)(2,1)}, u32[]{:S(2)}) copy-start(bf16[128,128]{1,0:T(8,128)(2,1)} %param.14) | copy-start | bytes 98308
  2.7 14.2 %copy-start.3 = (bf16[128,128]{1,0:T(8,128)(2,1)S(1)}, bf16[128,128]{1,0:T(8,128)(2,1)}, u32[]{:S(2)}) copy-start(bf16[128,128]{1,0:T(8,128)(2,1)} %param.15) | copy-start | bytes 98308
  2.7 7.7 %collective-permute-start = (bf16[4,16,128]{2,1,0:T(8,128)(2,1)S(1)}, bf16[4,16,128]{2,1,0:T(8,128)(2,1)S(1)}, u32[]{:S(2)}, u32[]{:S(2)}) collective-permute-start(bf16[4,16,128]{2,1,0:T(8,128)(2,1)S(1)} %bitcast.32), channel_id=1, source_target_pairs={{0,2},{2,4},{4,6},{6,8},{8,10},{10,12},{12,14},{14,0},{1,3},{3,5},... | collective-permute-start | bytes 49160 | tf_op jit(solution)/shard_map/ppermute | solution.py:54
  5.7 11.3 %collective-permute-start.4 = (bf16[4,16,128]{2,1,0:T(8,128)(2,1)S(1)}, bf16[4,16,128]{2,1,0:T(8,128)(2,1)S(1)}, u32[]{:S(2)}, u32[]{:S(2)}) collective-permute-start(bf16[4,16,128]{2,1,0:T(8,128)(2,1)S(1)} %bitcast.33), channel_id=1, source_target_pairs={{0,14},{2,0},{4,2},{6,4},{8,6},{10,8},{12,10},{14,12},{1,15},{3,1}... | collective-permute-start | bytes 49160 | tf_op jit(solution)/shard_map/ppermute | solution.py:56
  10.5 6.4 %collective-permute-start.1 = (bf16[4,16,128]{2,1,0:T(8,128)(2,1)S(1)}, bf16[4,16,128]{2,1,0:T(8,128)(2,1)S(1)}, u32[]{:S(2)}, u32[]{:S(2)}) collective-permute-start(bf16[4,16,128]{2,1,0:T(8,128)(2,1)S(1)} %collective-permute-done), channel_id=1, source_target_pairs={{0,2},{2,4},{4,6},{6,8},{8,10},{10,12},{12,14},{14,0},{1,3},{3,5},... | collective-permute-start | bytes 49160 | tf_op jit(solution)/shard_map/ppermute | solution.py:54
  10.6 12.7 %copy-start.10 = (bf16[128,128]{1,0:T(8,128)(2,1)S(1)}, bf16[128,128]{1,0:T(8,128)(2,1)}, u32[]{:S(2)}) copy-start(bf16[128,128]{1,0:T(8,128)(2,1)} %param.18) | copy-start | bytes 98308
  16.9 6.4 %collective-permute-start.2 = (bf16[4,16,128]{2,1,0:T(8,128)(2,1)S(1)}, bf16[4,16,128]{2,1,0:T(8,128)(2,1)S(1)}, u32[]{:S(2)}, u32[]{:S(2)}) collective-permute-start(bf16[4,16,128]{2,1,0:T(8,128)(2,1)S(1)} %collective-permute-done.1), channel_id=1, source_target_pairs={{0,2},{2,4},{4,6},{6,8},{8,10},{10,12},{12,14},{14,0},{1,3},{3,5},... | collective-permute-start | bytes 49160 | tf_op jit(solution)/shard_map/ppermute | solution.py:54
  17.0 8.5 %collective-permute-start.5 = (bf16[4,16,128]{2,1,0:T(8,128)(2,1)S(1)}, bf16[4,16,128]{2,1,0:T(8,128)(2,1)S(1)}, u32[]{:S(2)}, u32[]{:S(2)}) collective-permute-start(bf16[4,16,128]{2,1,0:T(8,128)(2,1)S(1)} %collective-permute-done.4), channel_id=1, source_target_pairs={{0,14},{2,0},{4,2},{6,4},{8,6},{10,8},{12,10},{14,12},{1,15},{3,1}... | collective-permute-start | bytes 49160 | tf_op jit(solution)/shard_map/ppermute | solution.py:56
  23.3 7.0 %collective-permute-start.3 = (bf16[4,16,128]{2,1,0:T(8,128)(2,1)S(1)}, bf16[4,16,128]{2,1,0:T(8,128)(2,1)S(1)}, u32[]{:S(2)}, u32[]{:S(2)}) collective-permute-start(bf16[4,16,128]{2,1,0:T(8,128)(2,1)S(1)} %collective-permute-done.2), channel_id=1, source_target_pairs={{0,2},{2,4},{4,6},{6,8},{8,10},{10,12},{12,14},{14,0},{1,3},{3,5},... | collective-permute-start | bytes 49160 | tf_op jit(solution)/shard_map/ppermute | solution.py:54
  25.5 6.2 %collective-permute-start.6 = (bf16[4,16,128]{2,1,0:T(8,128)(2,1)S(1)}, bf16[4,16,128]{2,1,0:T(8,128)(2,1)S(1)}, u32[]{:S(2)}, u32[]{:S(2)}) collective-permute-start(bf16[4,16,128]{2,1,0:T(8,128)(2,1)S(1)} %collective-permute-done.5), channel_id=1, source_target_pairs={{0,14},{2,0},{4,2},{6,4},{8,6},{10,8},{12,10},{14,12},{1,15},{3,1}... | collective-permute-start | bytes 49160 | tf_op jit(solution)/shard_map/ppermute | solution.py:56
  36.6 0.7 %copy-start.7 = (f32[128]{0:T(128)S(1)}, f32[128]{0:T(128)}, u32[]{:S(2)}) copy-start(f32[128]{0:T(128)} %param.20) | copy-start | bytes 1540
  36.6 0.7 %copy-start.8 = (f32[128]{0:T(128)S(1)}, f32[128]{0:T(128)}, u32[]{:S(2)}) copy-start(f32[128]{0:T(128)} %param.19) | copy-start | bytes 1540
  36.9 0.8 %copy-start.4 = (bf16[128,128]{1,0:T(8,128)(2,1)S(1)}, bf16[128,128]{1,0:T(8,128)(2,1)}, u32[]{:S(2)}) copy-start(bf16[128,128]{1,0:T(8,128)(2,1)} %param.21) | copy-start | bytes 98308
